TPU v7x, 128 devices: a whole 4x4x4 slice. The times are simulated.
128 devices in a mesh: row: 8 (over y_lo, z), col: 16 (over y_hi, x, core).
Axes of the slice: x: 4, y: 4 (y_hi: 2, y_lo: 2; y = y_hi * 2 + y_lo), z: 4, core: 2. Of those that a mesh axis runs over, the one named last changes fastest.
Arguments:
- embedding: float32 [16384, 256], P(('row', 'col')), may hold values from -6 to 6
- seed_cluster: int32 [16384], P(('row', 'col')), may hold values from 0 to 127
Outputs:
- log_member: float32 [16384, 128], P(('row', 'col'))
All inputs are finite; a program needn't handle non-finite values.
Results may differ from a plain program's by a relative error of at most 0.0003.
Values sent between devices are 32-bit elements; how exact they have to be, the bound alone decides.
No kernel may reach another device: no remote copies, remote signals or barrier semaphores. Data moves between devices by JAX's collectives and lax.ppermute only.
A program may use at most 64 MiB of HBM per device.

v0:
```python
import jax
import jax.numpy as jnp
from jax import lax
from jax.sharding import Mesh
from jax.sharding import PartitionSpec as P

CLUSTER_COUNT = 128
SWEEPS = 2
COL = ("col_0", "col_1", "col_2")
ROW = ("row_0", "row_1")
ROW_COL = ("row_0", "row_1", "col_0", "col_1", "col_2")
ANNEAL_TEMP_VALUE = 0.02


def from_everyone(x, axis):
    copies = jnp.broadcast_to(x, (lax.axis_size(axis), *x.shape))
    return lax.all_to_all(copies, axis, split_axis=0, concat_axis=0, tiled=True)


def in_order(blocks, dim):
    shape = list(blocks.shape[1:])
    shape[dim] *= blocks.shape[0]
    return jnp.moveaxis(blocks, 0, dim).reshape(shape)


def gathered_by_axis(x, axes, dim):
    far, near = axes
    blocks = from_everyone(from_everyone(x, far), near)
    return in_order(blocks.swapaxes(0, 1).reshape(-1, *x.shape), dim)


def gather_directly(x, axis, dim):
    blocks = from_everyone(x, axis)
    return in_order(blocks, dim)


def padded_to(lines, peers):
    spare = -len(lines) % peers
    return jnp.pad(lines, [(0, spare)] + [(0, 0)] * (lines.ndim - 1))


def in_blocks(x, dim, peers):
    before, after = (x.shape[:dim], x.shape[dim + 1 :])
    return jnp.moveaxis(x.reshape(*before, peers, -1, *after), dim, 0)


def sent_and_summed(x, axis, dim):
    peers = lax.axis_size(axis)
    blocks = lax.all_to_all(in_blocks(x, dim, peers), axis, 0, 0, tiled=True)
    return jnp.sum(blocks, axis=0)


def sum_in_two_steps(x, axes, dim):
    far, near = axes
    own = sent_and_summed(in_blocks(x, dim, lax.axis_size(far)), near, dim + 1)
    return jnp.sum(lax.all_to_all(own, far, 0, 0, tiled=True), axis=0)


def total_of(x, axes):
    lines = x.reshape(-1, x.shape[-1])
    padded = padded_to(lines, lax.axis_size(axes[0]) * lax.axis_size(axes[1]))
    whole = gathered_by_axis(sum_in_two_steps(padded, axes, 0), axes, 0)
    return lax.slice_in_dim(whole, 0, len(lines)).reshape(x.shape)


def by_axis(x, axes):
    for axis in axes:
        x = lax.psum(x, axis)
    return x


def shards(embedding, seed_cluster):
    per_device = embedding.shape[0]
    row_coords = gathered_by_axis(embedding, (("col_0", "col_1"), "col_2"), 0)
    col_coords, col_seeds = (
        gather_directly(embedding, ROW, 0),
        gather_directly(seed_cluster, ROW, 0),
    )
    row_sq = jnp.sum(row_coords * row_coords, axis=1)
    col_sq = jnp.sum(col_coords * col_coords, axis=1)
    inner = jnp.dot(row_coords, col_coords.T, precision=lax.Precision.HIGHEST)
    distance = jnp.sqrt(row_sq[:, None] + col_sq[None, :] - 2.0 * inner + 1.0)
    cluster_labels = jnp.arange(CLUSTER_COUNT, dtype=jnp.int32)
    member_cols = (
        0.5 * (col_seeds[:, None] == cluster_labels[None, :]).astype(jnp.float32)
        + 0.5 / CLUSTER_COUNT
    )
    member_own = (
        0.5 * (seed_cluster[:, None] == cluster_labels[None, :]).astype(jnp.float32)
        + 0.5 / CLUSTER_COUNT
    )
    log_member = jnp.zeros((per_device, CLUSTER_COUNT), jnp.float32)
    for sweep in range(SWEEPS):
        columns = member_cols
        summed_weights = total_of(
            jnp.dot(distance, columns, precision=lax.Precision.HIGHEST),
            (("col_0", "col_1"), "col_2"),
        )
        attraction = lax.dynamic_slice_in_dim(
            summed_weights, lax.axis_index(COL) * per_device, per_device, 0
        )
        counts, cohesion = (
            by_axis(jnp.sum(member_own, axis=0), ROW_COL),
            by_axis(jnp.sum(member_own * attraction, axis=0), ROW_COL),
        )
        pair_energy = attraction / counts[None, :] - cohesion[None, :] / (
            2.0 * counts[None, :] ** 2
        )
        member_logits = -pair_energy / ANNEAL_TEMP_VALUE
        highest = jnp.max(member_logits, axis=1, keepdims=True)
        log_member = (
            member_logits
            - highest
            - jnp.log(jnp.sum(jnp.exp(member_logits - highest), axis=1, keepdims=True))
        )
        member_own = jnp.exp(log_member)
        if sweep + 1 < SWEEPS:
            member_cols = gather_directly(member_own, ROW, 0)
    return log_member


def solution(mesh):
    finer = Mesh(mesh.devices.reshape(2, 4, 2, 4, 2), ("row_0", "row_1", "col_0", "col_1", "col_2"))
    placed = (P(ROW_COL, None), P(ROW_COL))
    return jax.shard_map(
        shards, mesh=finer, in_specs=placed, out_specs=P(ROW_COL, None), check_vma=False
    )
```

profile of v0, /device:TPU:1, one launch (start us, length us, event | category | flops | bytes accessed | tf_op | source)
XLA Modules:
  0.0 247.6 jit_solution(4716282031314174073)
XLA Ops:
  2.0 23.8 %all_to_all.66 = f32[8,128,256]{2,1,0:T(8,128)S(1)} all-to-all(f32[8,128,256]{2,1,0:T(8,128)} %broadcast_in_dim.16), channel_id=1, replica_groups=mesh['row_0'=2,'row_1'=4,'col_0'=2,'col_1'=4,'col_2'=2] {'col_0','col_1'}, dimensions={0} | all-to-all | bytes 2097152 | tf_op jit(solution)/shard_map/all_to_all | solution.py:17
  26.0 6.9 %all_to_all.67 = f32[2,8,128,256]{3,2,1,0:T(8,128)S(1)} all-to-all(f32[2,8,128,256]{3,2,1,0:T(8,128)S(1)} %broadcast_in_dim.17), channel_id=1, replica_groups=mesh['row_0'=2,'row_1'=4,'col_0'=2,'col_1'=4,'col_2'=2] {'col_2'}, dimensions={0} | all-to-all | bytes 4194304 | tf_op jit(solution)/shard_map/all_to_all | solution.py:17
  32.9 5.1 %all-to-all-start.2 = ((f32[8,128,256]{2,1,0:T(8,128)}), f32[8,128,256]{2,1,0:T(8,128)S(1)}, u32[]{:S(2)}, u32[]{:S(2)}) async-start(f32[8,128,256]{2,1,0:T(8,128)} %broadcast_in_dim.16), calls=%async_computation.2 | async-start | bytes 2097152 | tf_op jit(solution)/shard_map/all_to_all | solution.py:17
  40.0 13.0 %all-to-all-done.2 = f32[8,128,256]{2,1,0:T(8,128)S(1)} async-done(((f32[8,128,256]{2,1,0:T(8,128)}), f32[8,128,256]{2,1,0:T(8,128)S(1)}, u32[]{:S(2)}, u32[]{:S(2)}) %all-to-all-start.2) | async-done | bytes 1048608 | tf_op jit(solution)/shard_map/all_to_all | solution.py:17
  57.5 13.6 %add_sqrt_fusion = f32[2048,1024]{1,0:T(8,128)} fusion(f32[2048,256]{1,0:T(8,128)} %bitcast.38, f32[1024,256]{1,0:T(8,128)S(1)} %bitcast.35, f32[1024]{0:T(1024)S(1)} %bitcast.50, f32[2048]{0:T(1024)S(1)} %bitcast.49), kind=kOutput, calls=%fused_computation | convolution fusion | flops 6450839552 | bytes 11546624 | tf_op jit(solution)/shard_map/dot_general | solution.py:81
  71.1 9.2 %fusion.1 = f32[2048,128]{1,0:T(8,128)S(1)} fusion(f32[2048,1024]{1,0:T(8,128)} %add_sqrt_fusion, s32[1024]{0:T(1024)S(1)} %bitcast.48), kind=kOutput, calls=%fused_computation.6 | convolution fusion | flops 3221618688 | bytes 9441280 | tf_op jit(solution)/shard_map/dot_general | solution.py:96
  80.4 5.0 %all_to_all.68 = f32[2,8,128,128]{3,2,1,0:T(8,128)S(1)} all-to-all(f32[2,8,128,128]{3,2,1,0:T(8,128)S(1)} %bitcast.36), channel_id=1, replica_groups=mesh['row_0'=2,'row_1'=4,'col_0'=2,'col_1'=4,'col_2'=2] {'col_2'}, dimensions={0} | all-to-all | bytes 2097152 | tf_op jit(solution)/shard_map/all_to_all | solution.py:49
  85.4 13.9 %all_to_all.69 = f32[8,128,128]{2,1,0:T(8,128)S(1)} all-to-all(f32[8,128,128]{2,1,0:T(8,128)S(1)} %reduce_sum.110), channel_id=1, replica_groups=mesh['row_0'=2,'row_1'=4,'col_0'=2,'col_1'=4,'col_2'=2] {'col_0','col_1'}, dimensions={0} | all-to-all | bytes 1048576 | tf_op jit(solution)/shard_map/all_to_all | solution.py:56
  103.8 11.4 %all-to-all-done.6 = f32[8,128,128]{2,1,0:T(8,128)S(1)} async-done(((f32[8,128,128]{2,1,0:T(8,128)}), f32[8,128,128]{2,1,0:T(8,128)S(1)}, u32[]{:S(2)}, u32[]{:S(2)}) %all-to-all-start.6) | async-done | bytes 524320 | tf_op jit(solution)/shard_map/all_to_all | solution.py:17
  115.3 5.3 %all_to_all.70 = f32[2,8,128,128]{3,2,1,0:T(8,128)S(1)} all-to-all(f32[2,8,128,128]{3,2,1,0:T(8,128)S(1)} %broadcast_in_dim.20), channel_id=1, replica_groups=mesh['row_0'=2,'row_1'=4,'col_0'=2,'col_1'=4,'col_2'=2] {'col_2'}, dimensions={0} | all-to-all | bytes 2097152 | tf_op jit(solution)/shard_map/all_to_all | solution.py:17
  125.0 8.4 %all-reduce.3 = (f32[128]{0:T(128)S(1)}, f32[128]{0:T(128)S(1)}) all-reduce(f32[128]{0:T(128)S(1)} %get-tuple-element.27, f32[128]{0:T(128)S(1)} %get-tuple-element.28), channel_id=1, replica_groups=mesh['row_0'=2,'row_1'=4,'col_0'=2,'col_1'=4,'col_2'=2] {'row_1'}, use_global_device_ids=true, to_apply=%region_12.13 | all-reduce | flops 256 | bytes 2048 | tf_op jit(solution)/shard_map/psum | solution.py:68
  133.5 5.3 %all-reduce.7 = (f32[128]{0:T(128)S(1)}, f32[128]{0:T(128)S(1)}) all-reduce(f32[128]{0:T(128)S(1)} %get-tuple-element.15, f32[128]{0:T(128)S(1)} %get-tuple-element.16), channel_id=1, replica_groups=mesh['row_0'=2,'row_1'=4,'col_0'=2,'col_1'=4,'col_2'=2] {'col_0'}, use_global_device_ids=true, to_apply=%region_13.14 | all-reduce | flops 256 | bytes 2048 | tf_op jit(solution)/shard_map/psum | solution.py:68
  138.7 6.6 %all-reduce.1 = (f32[128]{0:T(128)S(1)}, f32[128]{0:T(128)S(1)}) all-reduce(f32[128]{0:T(128)S(1)} %get-tuple-element.23, f32[128]{0:T(128)S(1)} %get-tuple-element.24), channel_id=1, replica_groups=mesh['row_0'=2,'row_1'=4,'col_0'=2,'col_1'=4,'col_2'=2] {'col_1'}, use_global_device_ids=true, to_apply=%region_14.15 | all-reduce | flops 256 | bytes 2048 | tf_op jit(solution)/shard_map/psum | solution.py:68
  145.3 9.0 %all-reduce.5 = (f32[128]{0:T(128)S(1)}, f32[128]{0:T(128)S(1)}) all-reduce(f32[128]{0:T(128)S(1)} %get-tuple-element.11, f32[128]{0:T(128)S(1)} %get-tuple-element.12), channel_id=1, replica_groups=mesh['row_0'=2,'row_1'=4,'col_0'=2,'col_1'=4,'col_2'=2] {'col_2'}, use_global_device_ids=true, to_apply=%region_15.16 | all-reduce | flops 256 | bytes 2048 | tf_op jit(solution)/shard_map/psum | solution.py:68
  154.8 11.6 %all_to_all.71 = f32[8,128,128]{2,1,0:T(8,128)S(1)} all-to-all(f32[8,128,128]{2,1,0:T(8,128)S(1)} %broadcast_in_dim.21), channel_id=1, replica_groups=mesh['row_0'=2,'row_1'=4,'col_0'=2,'col_1'=4,'col_2'=2] {'row_0','row_1'}, dimensions={0} | all-to-all | bytes 1048576 | tf_op jit(solution)/shard_map/all_to_all | solution.py:17
  166.4 9.1 %convolution_bitcast_fusion = f32[2,8,128,128]{3,2,0,1:T(8,128)S(1)} fusion(f32[8,2,128,1024]{3,2,1,0:T(8,128)} %bitcast.33, f32[1024,128,1,1]{1,0,3,2:T(8,128)S(1)} %bitcast.37), kind=kOutput, calls=%fused_computation.3 | convolution fusion | flops 3221225472 | bytes 9961472 | tf_op jit(solution)/shard_map/dot_general | solution.py:96
  175.6 6.4 %all_to_all.72 = f32[2,8,128,128]{3,2,1,0:T(8,128)S(1)} all-to-all(f32[2,8,128,128]{3,2,1,0:T(8,128)S(1)} %copy.14), channel_id=1, replica_groups=mesh['row_0'=2,'row_1'=4,'col_0'=2,'col_1'=4,'col_2'=2] {'col_2'}, dimensions={0} | all-to-all | bytes 2097152 | tf_op jit(solution)/shard_map/all_to_all | solution.py:49
  182.0 13.8 %all_to_all.73 = f32[8,128,128]{2,1,0:T(8,128)S(1)} all-to-all(f32[8,128,128]{2,1,0:T(8,128)S(1)} %reduce_sum.115), channel_id=1, replica_groups=mesh['row_0'=2,'row_1'=4,'col_0'=2,'col_1'=4,'col_2'=2] {'col_0','col_1'}, dimensions={0} | all-to-all | bytes 1048576 | tf_op jit(solution)/shard_map/all_to_all | solution.py:56
  195.9 12.7 %all_to_all.74 = f32[8,128,128]{2,1,0:T(8,128)S(1)} all-to-all(f32[8,128,128]{2,1,0:T(8,128)S(1)} %broadcast_in_dim.22), channel_id=1, replica_groups=mesh['row_0'=2,'row_1'=4,'col_0'=2,'col_1'=4,'col_2'=2] {'col_0','col_1'}, dimensions={0} | all-to-all | bytes 1048576 | tf_op jit(solution)/shard_map/all_to_all | solution.py:17
  208.8 6.4 %all_to_all.75 = f32[2,8,128,128]{3,2,1,0:T(8,128)S(1)} all-to-all(f32[2,8,128,128]{3,2,1,0:T(8,128)S(1)} %broadcast_in_dim.23), channel_id=1, replica_groups=mesh['row_0'=2,'row_1'=4,'col_0'=2,'col_1'=4,'col_2'=2] {'col_2'}, dimensions={0} | all-to-all | bytes 2097152 | tf_op jit(solution)/shard_map/all_to_all | solution.py:17
  219.2 6.5 %all-reduce.2 = (f32[128]{0:T(128)S(1)}, f32[128]{0:T(128)S(1)}) all-reduce(f32[128]{0:T(128)S(1)} %get-tuple-element.25, f32[128]{0:T(128)S(1)} %get-tuple-element.26), channel_id=1, replica_groups=mesh['row_0'=2,'row_1'=4,'col_0'=2,'col_1'=4,'col_2'=2] {'row_1'}, use_global_device_ids=true, to_apply=%region_28.29 | all-reduce | flops 256 | bytes 2048 | tf_op jit(solution)/shard_map/psum | solution.py:68
  225.7 5.3 %all-reduce.6 = (f32[128]{0:T(128)S(1)}, f32[128]{0:T(128)S(1)}) all-reduce(f32[128]{0:T(128)S(1)} %get-tuple-element.13, f32[128]{0:T(128)S(1)} %get-tuple-element.14), channel_id=1, replica_groups=mesh['row_0'=2,'row_1'=4,'col_0'=2,'col_1'=4,'col_2'=2] {'col_0'}, use_global_device_ids=true, to_apply=%region_29.30 | all-reduce | flops 256 | bytes 2048 | tf_op jit(solution)/shard_map/psum | solution.py:68
  230.9 6.8 %all-reduce = (f32[128]{0:T(128)S(1)}, f32[128]{0:T(128)S(1)}) all-reduce(f32[128]{0:T(128)S(1)} %get-tuple-element.21, f32[128]{0:T(128)S(1)} %get-tuple-element.22), channel_id=1, replica_groups=mesh['row_0'=2,'row_1'=4,'col_0'=2,'col_1'=4,'col_2'=2] {'col_1'}, use_global_device_ids=true, to_apply=%region_30.31 | all-reduce | flops 256 | bytes 2048 | tf_op jit(solution)/shard_map/psum | solution.py:68
  237.7 8.8 %all-reduce.4 = (f32[128]{0:T(128)S(1)}, f32[128]{0:T(128)S(1)}) all-reduce(f32[128]{0:T(128)S(1)} %get-tuple-element.9, f32[128]{0:T(128)S(1)} %get-tuple-element.10), channel_id=1, replica_groups=mesh['row_0'=2,'row_1'=4,'col_0'=2,'col_1'=4,'col_2'=2] {'col_2'}, use_global_device_ids=true, to_apply=%region_31.32 | all-reduce | flops 256 | bytes 2048 | tf_op jit(solution)/shard_map/psum | solution.py:68
  (38 shorter events, 23.6 us)
Async XLA Ops:
  25.8 27.2 %copy-start = (s32[128]{0:T(128)S(1)}, s32[128]{0:T(128)}, u32[]{:S(2)}) copy-start(s32[128]{0:T(128)} %param.3) | copy-start | bytes 1540
  32.9 20.1 %all-to-all-start.2 = ((f32[8,128,256]{2,1,0:T(8,128)}), f32[8,128,256]{2,1,0:T(8,128)S(1)}, u32[]{:S(2)}, u32[]{:S(2)}) async-start(f32[8,128,256]{2,1,0:T(8,128)} %broadcast_in_dim.16), calls=%async_computation.2 | async-start | bytes 2097152 | tf_op jit(solution)/shard_map/all_to_all | solution.py:17
  53.6 17.5 %all-to-all-start.3 = ((s32[8,1,128]{2,1,0:T(1,128)}), s32[8,1,128]{2,1,0:T(1,128)S(1)}, u32[]{:S(2)}, u32[]{:S(2)}) async-start(s32[8,1,128]{2,1,0:T(1,128)} %broadcast_in_dim.18), calls=%async_computation.3 | async-start | bytes 8192 | tf_op jit(solution)/shard_map/all_to_all | solution.py:17
  100.3 14.9 %all-to-all-start.6 = ((f32[8,128,128]{2,1,0:T(8,128)}), f32[8,128,128]{2,1,0:T(8,128)S(1)}, u32[]{:S(2)}, u32[]{:S(2)}) async-start(f32[8,128,128]{2,1,0:T(8,128)} %broadcast_in_dim.19), calls=%async_computation.6 | async-start | bytes 1048576 | tf_op jit(solution)/shard_map/all_to_all | solution.py:17
where the time goes:
time: 249 us; the launch traced here: 248 us
  blocking collectives  170 us (68%)
  matrix products  31.9 us (13%)
  waiting for transfers between devices  24.4 us (10%)
  starting transfers between devices  12.3 us (5%)
  local copies, waits for them, and re-layouts  5.86 us (2%)
  other arithmetic  2.54 us (1%)
    all_to_all x6, blocking collectives, from_everyone(): return lax.all_to_all(copies, axis, split_axis=0, concat_axis=0, tiled=True)  66.7 us
    psum x10, blocking collectives, by_axis(): x = lax.psum(x, axis)  64.7 us
    all_to_all x2, blocking collectives, sum_in_two_steps(): return jnp.sum(lax.all_to_all(own, far, 0, 0, tiled=True), axis=0)  27.7 us
    all_to_all x3, waiting for transfers between devices, from_everyone(): return lax.all_to_all(copies, axis, split_axis=0, concat_axis=0, tiled=True)  24.4 us
    dot_general x2, matrix products, shards(): jnp.dot(distance, columns, precision=lax.Precision.HIGHEST)  18.3 us
    dot_general x1, matrix products, shards(): inner = jnp.dot(row_coords, col_coords.T, precision=lax.Precision.HIGHEST)  13.6 us
    all_to_all x3, starting transfers between devices, from_everyone(): return lax.all_to_all(copies, axis, split_axis=0, concat_axis=0, tiled=True)  12.3 us
    all_to_all x2, blocking collectives, sent_and_summed(): blocks = lax.all_to_all(in_blocks(x, dim, peers), axis, 0, 0, tiled=True)  11.3 us
  transfers between devices with their start and end apart: 3, of which 2 were waited for; matrix products, arithmetic and copies ran while one was open for 6% of the time, Pallas kernels for 0%

commit v1 on v0

--- a/solution.py
+++ b/solution.py
@@ -65,7 +65,7 @@
 
 def by_axis(x, axes):
     for axis in axes:
-        x = lax.psum(x, axis)
+        x = jnp.sum(lax.all_gather(x, axis), axis=0)
     return x
 
 

time: 249 us -> 297 us (1.19)
  blocking collectives: 170 us -> 219 us
    all_gather x0 -> x20, blocking collectives: none -> 112 us  [by_axis(): x = jnp.sum(lax.all_gather(x, axis), axis=0)]
    psum x10 -> x0, blocking collectives: 64.7 us -> none  [by_axis(): x = lax.psum(x, axis)]
  transfers between devices with their start and end apart: 3 -> 3, of which waited for: 2 -> 2; matrix products, arithmetic and copies ran while one was open for 6% -> 5% of each run, Pallas kernels for 0% -> 0%
where the time goes in v1:
time: 297 us; the launch traced here: 296 us
  blocking collectives  219 us (74%)
  matrix products  31.9 us (11%)
  waiting for transfers between devices  24.4 us (8%)
  starting transfers between devices  12.3 us (4%)
  local copies, waits for them, and re-layouts  5.86 us (2%)
    all_gather x20, blocking collectives, by_axis(): x = jnp.sum(lax.all_gather(x, axis), axis=0)  112 us
    all_to_all x6, blocking collectives, from_everyone(): return lax.all_to_all(copies, axis, split_axis=0, concat_axis=0, tiled=True)  67.8 us
    all_to_all x2, blocking collectives, sum_in_two_steps(): return jnp.sum(lax.all_to_all(own, far, 0, 0, tiled=True), axis=0)  27.7 us
    all_to_all x3, waiting for transfers between devices, from_everyone(): return lax.all_to_all(copies, axis, split_axis=0, concat_axis=0, tiled=True)  24.4 us
    dot_general x2, matrix products, shards(): jnp.dot(distance, columns, precision=lax.Precision.HIGHEST)  18.3 us
    dot_general x1, matrix products, shards(): inner = jnp.dot(row_coords, col_coords.T, precision=lax.Precision.HIGHEST)  13.6 us
    all_to_all x3, starting transfers between devices, from_everyone(): return lax.all_to_all(copies, axis, split_axis=0, concat_axis=0, tiled=True)  12.3 us
    all_to_all x2, blocking collectives, sent_and_summed(): blocks = lax.all_to_all(in_blocks(x, dim, peers), axis, 0, 0, tiled=True)  11.4 us
  transfers between devices with their start and end apart: 3, of which 2 were waited for; matrix products, arithmetic and copies ran while one was open for 5% of the time, Pallas kernels for 0%

profile of v1, /device:TPU:1, one launch (start us, length us, event | category | flops | bytes accessed | tf_op | source)
XLA Modules:
  0.0 296.1 jit_solution(1828818264624240424)
XLA Ops:
  2.0 23.8 %all_to_all.66 = f32[8,128,256]{2,1,0:T(8,128)S(1)} all-to-all(f32[8,128,256]{2,1,0:T(8,128)} %broadcast_in_dim.16), channel_id=1, replica_groups=mesh['row_0'=2,'row_1'=4,'col_0'=2,'col_1'=4,'col_2'=2] {'col_0','col_1'}, dimensions={0} | all-to-all | bytes 2097152 | tf_op jit(solution)/shard_map/all_to_all | solution.py:17
  26.0 6.9 %all_to_all.67 = f32[2,8,128,256]{3,2,1,0:T(8,128)S(1)} all-to-all(f32[2,8,128,256]{3,2,1,0:T(8,128)S(1)} %broadcast_in_dim.17), channel_id=1, replica_groups=mesh['row_0'=2,'row_1'=4,'col_0'=2,'col_1'=4,'col_2'=2] {'col_2'}, dimensions={0} | all-to-all | bytes 4194304 | tf_op jit(solution)/shard_map/all_to_all | solution.py:17
  40.0 13.0 %all-to-all-done.2 = f32[8,128,256]{2,1,0:T(8,128)S(1)} async-done(((f32[8,128,256]{2,1,0:T(8,128)}), f32[8,128,256]{2,1,0:T(8,128)S(1)}, u32[]{:S(2)}, u32[]{:S(2)}) %all-to-all-start.2) | async-done | bytes 1048608 | tf_op jit(solution)/shard_map/all_to_all | solution.py:17
  57.5 13.6 %add_sqrt_fusion = f32[2048,1024]{1,0:T(8,128)} fusion(f32[2048,256]{1,0:T(8,128)} %bitcast.58, f32[1024,256]{1,0:T(8,128)S(1)} %bitcast.55, f32[1024]{0:T(1024)S(1)} %bitcast.70, f32[2048]{0:T(1024)S(1)} %bitcast.69), kind=kOutput, calls=%fused_computation | convolution fusion | flops 6450839552 | bytes 11546624 | tf_op jit(solution)/shard_map/dot_general | solution.py:81
  71.1 9.2 %fusion.1 = f32[2048,128]{1,0:T(8,128)S(1)} fusion(f32[2048,1024]{1,0:T(8,128)} %add_sqrt_fusion, s32[1024]{0:T(1024)S(1)} %bitcast.68), kind=kOutput, calls=%fused_computation.6 | convolution fusion | flops 3221618688 | bytes 9441280 | tf_op jit(solution)/shard_map/dot_general | solution.py:96
  85.4 13.9 %all_to_all.69 = f32[8,128,128]{2,1,0:T(8,128)S(1)} all-to-all(f32[8,128,128]{2,1,0:T(8,128)S(1)} %reduce_sum.290), channel_id=1, replica_groups=mesh['row_0'=2,'row_1'=4,'col_0'=2,'col_1'=4,'col_2'=2] {'col_0','col_1'}, dimensions={0} | all-to-all | bytes 1048576 | tf_op jit(solution)/shard_map/all_to_all | solution.py:56
  103.8 11.4 %all-to-all-done.6 = f32[8,128,128]{2,1,0:T(8,128)S(1)} async-done(((f32[8,128,128]{2,1,0:T(8,128)}), f32[8,128,128]{2,1,0:T(8,128)S(1)}, u32[]{:S(2)}, u32[]{:S(2)}) %all-to-all-start.6) | async-done | bytes 524320 | tf_op jit(solution)/shard_map/all_to_all | solution.py:17
  124.3 7.6 %all-gather.26 = f32[4,1,128]{2,1,0:T(1,128)S(1)} all-gather(f32[1,1,128]{2,1,0:T(1,128)S(1)} %bitcast.71), channel_id=8, replica_groups=mesh['row_0'=2,'row_1'=4,'col_0'=2,'col_1'=4,'col_2'=2] {'row_1'}, dimensions={0}, use_global_device_ids=true | all-gather | bytes 2560 | tf_op jit(solution)/shard_map/all_gather | solution.py:68
  136.6 5.8 %all-gather.28 = f32[4,1,128]{2,1,0:T(1,128)S(1)} all-gather(f32[1,1,128]{2,1,0:T(1,128)S(1)} %bitcast.72), channel_id=10, replica_groups=mesh['row_0'=2,'row_1'=4,'col_0'=2,'col_1'=4,'col_2'=2] {'col_1'}, dimensions={0}, use_global_device_ids=true | all-gather | bytes 2560 | tf_op jit(solution)/shard_map/all_gather | solution.py:68
  142.4 8.2 %all-gather.29 = f32[2,1,128]{2,1,0:T(1,128)S(1)} all-gather(f32[1,1,128]{2,1,0:T(1,128)S(1)} %bitcast.84), channel_id=11, replica_groups=mesh['row_0'=2,'row_1'=4,'col_0'=2,'col_1'=4,'col_2'=2] {'col_2'}, dimensions={0}, use_global_device_ids=true | all-gather | bytes 1536 | tf_op jit(solution)/shard_map/all_gather | solution.py:68
  163.4 6.0 %all-gather.23 = f32[4,1,128]{2,1,0:T(1,128)S(1)} all-gather(f32[1,1,128]{2,1,0:T(1,128)S(1)} %bitcast.74), channel_id=5, replica_groups=mesh['row_0'=2,'row_1'=4,'col_0'=2,'col_1'=4,'col_2'=2] {'col_1'}, dimensions={0}, use_global_device_ids=true | all-gather | bytes 2560 | tf_op jit(solution)/shard_map/all_gather | solution.py:68
  169.5 8.0 %all-gather.24 = f32[2,1,128]{2,1,0:T(1,128)S(1)} all-gather(f32[1,1,128]{2,1,0:T(1,128)S(1)} %bitcast.86), channel_id=6, replica_groups=mesh['row_0'=2,'row_1'=4,'col_0'=2,'col_1'=4,'col_2'=2] {'col_2'}, dimensions={0}, use_global_device_ids=true | all-gather | bytes 1536 | tf_op jit(solution)/shard_map/all_gather | solution.py:68
  178.0 12.7 %all_to_all.71 = f32[8,128,128]{2,1,0:T(8,128)S(1)} all-to-all(f32[8,128,128]{2,1,0:T(8,128)S(1)} %broadcast_in_dim.21), channel_id=1, replica_groups=mesh['row_0'=2,'row_1'=4,'col_0'=2,'col_1'=4,'col_2'=2] {'row_0','row_1'}, dimensions={0} | all-to-all | bytes 1048576 | tf_op jit(solution)/shard_map/all_to_all | solution.py:17
  190.7 9.1 %convolution_bitcast_fusion = f32[2,8,128,128]{3,2,0,1:T(8,128)S(1)} fusion(f32[8,2,128,1024]{3,2,1,0:T(8,128)} %bitcast.53, f32[1024,128,1,1]{1,0,3,2:T(8,128)S(1)} %bitcast.57), kind=kOutput, calls=%fused_computation.3 | convolution fusion | flops 3221225472 | bytes 9961472 | tf_op jit(solution)/shard_map/dot_general | solution.py:96
  199.8 6.4 %all_to_all.72 = f32[2,8,128,128]{3,2,1,0:T(8,128)S(1)} all-to-all(f32[2,8,128,128]{3,2,1,0:T(8,128)S(1)} %copy.14), channel_id=1, replica_groups=mesh['row_0'=2,'row_1'=4,'col_0'=2,'col_1'=4,'col_2'=2] {'col_2'}, dimensions={0} | all-to-all | bytes 2097152 | tf_op jit(solution)/shard_map/all_to_all | solution.py:49
  206.4 13.8 %all_to_all.73 = f32[8,128,128]{2,1,0:T(8,128)S(1)} all-to-all(f32[8,128,128]{2,1,0:T(8,128)S(1)} %reduce_sum.305), channel_id=1, replica_groups=mesh['row_0'=2,'row_1'=4,'col_0'=2,'col_1'=4,'col_2'=2] {'col_0','col_1'}, dimensions={0} | all-to-all | bytes 1048576 | tf_op jit(solution)/shard_map/all_to_all | solution.py:56
  220.3 12.7 %all_to_all.74 = f32[8,128,128]{2,1,0:T(8,128)S(1)} all-to-all(f32[8,128,128]{2,1,0:T(8,128)S(1)} %broadcast_in_dim.22), channel_id=1, replica_groups=mesh['row_0'=2,'row_1'=4,'col_0'=2,'col_1'=4,'col_2'=2] {'col_0','col_1'}, dimensions={0} | all-to-all | bytes 1048576 | tf_op jit(solution)/shard_map/all_to_all | solution.py:17
  233.1 6.4 %all_to_all.75 = f32[2,8,128,128]{3,2,1,0:T(8,128)S(1)} all-to-all(f32[2,8,128,128]{3,2,1,0:T(8,128)S(1)} %broadcast_in_dim.23), channel_id=1, replica_groups=mesh['row_0'=2,'row_1'=4,'col_0'=2,'col_1'=4,'col_2'=2] {'col_2'}, dimensions={0} | all-to-all | bytes 2097152 | tf_op jit(solution)/shard_map/all_to_all | solution.py:17
  242.8 5.7 %all-gather.36 = f32[4,1,128]{2,1,0:T(1,128)S(1)} all-gather(f32[1,1,128]{2,1,0:T(1,128)S(1)} %bitcast.75), channel_id=18, replica_groups=mesh['row_0'=2,'row_1'=4,'col_0'=2,'col_1'=4,'col_2'=2] {'row_1'}, dimensions={0}, use_global_device_ids=true | all-gather | bytes 2560 | tf_op jit(solution)/shard_map/all_gather | solution.py:68
  253.1 6.0 %all-gather.38 = f32[4,1,128]{2,1,0:T(1,128)S(1)} all-gather(f32[1,1,128]{2,1,0:T(1,128)S(1)} %bitcast.76), channel_id=20, replica_groups=mesh['row_0'=2,'row_1'=4,'col_0'=2,'col_1'=4,'col_2'=2] {'col_1'}, dimensions={0}, use_global_device_ids=true | all-gather | bytes 2560 | tf_op jit(solution)/shard_map/all_gather | solution.py:68
  259.1 8.2 %all-gather.39 = f32[2,1,128]{2,1,0:T(1,128)S(1)} all-gather(f32[1,1,128]{2,1,0:T(1,128)S(1)} %bitcast.88), channel_id=21, replica_groups=mesh['row_0'=2,'row_1'=4,'col_0'=2,'col_1'=4,'col_2'=2] {'col_2'}, dimensions={0}, use_global_device_ids=true | all-gather | bytes 1536 | tf_op jit(solution)/shard_map/all_gather | solution.py:68
  270.4 6.1 %all-gather.31 = f32[4,1,128]{2,1,0:T(1,128)S(1)} all-gather(f32[1,1,128]{2,1,0:T(1,128)S(1)} %bitcast.77), channel_id=13, replica_groups=mesh['row_0'=2,'row_1'=4,'col_0'=2,'col_1'=4,'col_2'=2] {'row_1'}, dimensions={0}, use_global_device_ids=true | all-gather | bytes 2560 | tf_op jit(solution)/shard_map/all_gather | solution.py:68
  281.1 5.8 %all-gather.33 = f32[4,1,128]{2,1,0:T(1,128)S(1)} all-gather(f32[1,1,128]{2,1,0:T(1,128)S(1)} %bitcast.78), channel_id=15, replica_groups=mesh['row_0'=2,'row_1'=4,'col_0'=2,'col_1'=4,'col_2'=2] {'col_1'}, dimensions={0}, use_global_device_ids=true | all-gather | bytes 2560 | tf_op jit(solution)/shard_map/all_gather | solution.py:68
  286.9 8.1 %all-gather.34 = f32[2,1,128]{2,1,0:T(1,128)S(1)} all-gather(f32[1,1,128]{2,1,0:T(1,128)S(1)} %bitcast.90), channel_id=16, replica_groups=mesh['row_0'=2,'row_1'=4,'col_0'=2,'col_1'=4,'col_2'=2] {'col_2'}, dimensions={0}, use_global_device_ids=true | all-gather | bytes 1536 | tf_op jit(solution)/shard_map/all_gather | solution.py:68
  (68 shorter events, 67.6 us)
Async XLA Ops:
  25.8 27.2 %copy-start = (s32[128]{0:T(128)S(1)}, s32[128]{0:T(128)}, u32[]{:S(2)}) copy-start(s32[128]{0:T(128)} %param.3) | copy-start | bytes 1540
  32.9 20.1 %all-to-all-start.2 = ((f32[8,128,256]{2,1,0:T(8,128)}), f32[8,128,256]{2,1,0:T(8,128)S(1)}, u32[]{:S(2)}, u32[]{:S(2)}) async-start(f32[8,128,256]{2,1,0:T(8,128)} %broadcast_in_dim.16), calls=%async_computation.2 | async-start | bytes 2097152 | tf_op jit(solution)/shard_map/all_to_all | solution.py:17
  53.6 17.5 %all-to-all-start.3 = ((s32[8,1,128]{2,1,0:T(1,128)}), s32[8,1,128]{2,1,0:T(1,128)S(1)}, u32[]{:S(2)}, u32[]{:S(2)}) async-start(s32[8,1,128]{2,1,0:T(1,128)} %broadcast_in_dim.18), calls=%async_computation.3 | async-start | bytes 8192 | tf_op jit(solution)/shard_map/all_to_all | solution.py:17
  100.3 14.9 %all-to-all-start.6 = ((f32[8,128,128]{2,1,0:T(8,128)}), f32[8,128,128]{2,1,0:T(8,128)S(1)}, u32[]{:S(2)}, u32[]{:S(2)}) async-start(f32[8,128,128]{2,1,0:T(8,128)} %broadcast_in_dim.19), calls=%async_computation.6 | async-start | bytes 1048576 | tf_op jit(solution)/shard_map/all_to_all | solution.py:17
